TPU v7x, 512 devices: a whole 4x8x8 slice. The times are simulated.
512 devices in a mesh: ens: 16 (over x, y_lo), lat: 32 (over y_hi, z, core).
Axes of the slice: x: 4, y: 8 (y_hi: 2, y_lo: 4; y = y_hi * 4 + y_lo), z: 8, core: 2. Of those that a mesh axis runs over, the one named last changes fastest.
Arguments:
- features: bfloat16 [128, 128, 128], P('lat'), may hold values from -6 to 6
- random_perturbation: bfloat16 [16, 128, 128, 128], P('ens', 'lat'), may hold values from -6 to 6
- observed_truth: float32 [69, 128, 128], P(None, 'lat'), may hold values from -6 to 6
- stencil_taps: float32 [49, 128], replicated, may hold values from -0.875 to 0.875
- affine_factor: float32 [128], replicated, may hold values from 0.5 to 1.5
- widen_matrix: bfloat16 [512, 128], P('lat'), may hold values from -0.5 to 0.5
- shrink_matrix: bfloat16 [512, 128], P('lat'), may hold values from -0.25 to 0.25
- readout_matrix: bfloat16 [69, 128], replicated, may hold values from -0.5 to 0.5
Outputs:
- crps_score: float32 [], replicated
- stencil_taps_sensitivity: float32 [49, 128], replicated
- affine_factor_sensitivity: float32 [128], replicated
- widen_matrix_sensitivity: float32 [512, 128], P('lat')
- shrink_matrix_sensitivity: float32 [512, 128], P('lat')
- readout_matrix_sensitivity: float32 [69, 128], replicated
- sample_outlook: bfloat16 [16, 69, 128, 128], P('ens', None, 'lat')
- sample_average_spread: float32 [16, 69, 128, 128], P('ens', None, 'lat')
All inputs are finite; a program needn't handle non-finite values.
Results may differ from a plain program's by a relative error of at most 0.0024.
The roundings to bfloat16 on the way count: a program that leaves them out, or rounds other values in their place, can miss the bound.
Values may be sent and summed in bfloat16 or wider, within the bound.
No kernel may reach another device: no remote copies, remote signals or barrier semaphores. Data moves between devices by JAX's collectives and lax.ppermute only.
A program may use at most 64 MiB of HBM per device.

v0:
```python
import math
import jax
import jax.numpy as jnp
from jax import lax
from jax.sharding import PartitionSpec as P

STENCIL_SIDE = 7
SQRT_TWO_PI = 0.7978845608028654
CUBIC = 0.044715
EPSILON = 1e-06
SMOOTHING = 0.01


def extended(cells, sides, width):
    for axis, dim in sides:
        count = lax.axis_size(axis)
        ends = count - 1
        head = lax.slice_in_dim(cells, 0, width, axis=dim)
        tail = lax.slice_in_dim(cells, cells.shape[dim] - width, cells.shape[dim], axis=dim)
        cells = jnp.concatenate(
            [
                lax.ppermute(tail, axis, [(i, (i + 1) % count) for i in range(ends)]),
                cells,
                lax.ppermute(head, axis, [((i + 1) % count, i) for i in range(ends)]),
            ],
            axis=dim,
        )
    return cells


def smooth_magnitude(value):
    return jnp.sqrt(value * value + SMOOTHING)


def smooth_slope(value):
    return value * lax.rsqrt(value * value + SMOOTHING)


def gelu_tanh(northern_margin):
    return (
        0.5
        * northern_margin
        * (
            1.0
            + jnp.tanh(
                SQRT_TWO_PI
                * (northern_margin + CUBIC * northern_margin * northern_margin * northern_margin)
            )
        )
    )


def gelu_slope(northern_margin):
    inner = jnp.tanh(
        SQRT_TWO_PI
        * (northern_margin + CUBIC * northern_margin * northern_margin * northern_margin)
    )
    return 0.5 * (1.0 + inner) + 0.5 * northern_margin * (1.0 - inner * inner) * SQRT_TWO_PI * (
        1.0 + 3.0 * CUBIC * northern_margin * northern_margin
    )


def depthwise(margin_extended, stencil_taps, meridian_slab):
    half = STENCIL_SIDE // 2
    wide = margin_extended.astype(jnp.float32)
    axis_rows = wide.ndim - 3
    result = jnp.zeros(
        wide.shape[:axis_rows] + (meridian_slab,) + wide.shape[axis_rows + 1 :], jnp.float32
    )
    for offset_row in range(STENCIL_SIDE):
        band = lax.slice_in_dim(wide, offset_row, offset_row + meridian_slab, axis=axis_rows)
        for offset_col in range(STENCIL_SIDE):
            result = result + stencil_taps[offset_row * STENCIL_SIDE + offset_col] * jnp.roll(
                band, half - offset_col, axis=-2
            )
    return result


def kernel_grad(margin_extended, upstream, meridian_slab):
    half = STENCIL_SIDE // 2
    wide = margin_extended.astype(jnp.float32)
    axis_rows = wide.ndim - 3
    channels = upstream.shape[-1]
    taps = []
    for offset_row in range(STENCIL_SIDE):
        band = lax.slice_in_dim(wide, offset_row, offset_row + meridian_slab, axis=axis_rows)
        for offset_col in range(STENCIL_SIDE):
            shifted = jnp.roll(band, half - offset_col, axis=-2)
            taps.append(jnp.sum((upstream * shifted).reshape(-1, channels), axis=0))
    return jnp.stack(taps)


def normalize(depth_out):
    centre = jnp.mean(depth_out, axis=-1, keepdims=True)
    centred = depth_out - centre
    variance = jnp.mean(centred * centred, axis=-1, keepdims=True)
    reciprocal_spread = lax.rsqrt(variance + EPSILON)
    return (centred * reciprocal_spread, reciprocal_spread)


def pair_terms(carry, owned_subset, piece):

    def one_pair(totals, other):
        gap = owned_subset - other.astype(jnp.float32)[None]
        return ((totals[0] + smooth_magnitude(gap), totals[1] + smooth_slope(gap)), None)

    carry, ignored_entry = lax.scan(one_pair, carry, piece)
    return carry


def on_device(
    features,
    random_perturbation,
    observed_truth,
    stencil_taps,
    affine_factor,
    widen_matrix,
    shrink_matrix,
    readout_matrix,
):
    sample_count, meridian_slab, zonal_points, channels = random_perturbation.shape
    outlook_quantities = readout_matrix.shape[0]
    half = STENCIL_SIDE // 2
    latitudes = meridian_slab * lax.axis_size("lat")
    ensemble = sample_count * lax.axis_size("ens")
    point_tally = meridian_slab * zonal_points
    planar_map = (
        features[None].astype(jnp.float32) + random_perturbation.astype(jnp.float32)
    ).astype(jnp.bfloat16)
    margin_extended = extended(planar_map, (("lat", 1),), half)
    up_full, down_full = (
        lax.all_gather(widen_matrix, "lat", axis=0, tiled=True),
        lax.all_gather(shrink_matrix, "lat", axis=0, tiled=True),
    )
    depth_out = depthwise(margin_extended, stencil_taps, meridian_slab)
    factor_multiplied, reciprocal_spread = normalize(depth_out)
    standardized_activation = (
        (affine_factor * factor_multiplied)
        .astype(jnp.bfloat16)
        .reshape(sample_count * point_tally, channels)
    )
    northern_margin = lax.dot_general(
        standardized_activation,
        up_full,
        (((1,), (1,)), ((), ())),
        preferred_element_type=jnp.float32,
    )
    nonlinear_response = gelu_tanh(northern_margin).astype(jnp.bfloat16)
    mixed = jnp.dot(nonlinear_response, down_full, preferred_element_type=jnp.float32)
    skip_activation = (
        planar_map.reshape(sample_count * point_tally, channels).astype(jnp.float32) + mixed
    ).astype(jnp.bfloat16)
    residual_row_block = skip_activation.reshape(sample_count, point_tally, channels)
    sample_outlook = jnp.einsum(
        "au,blu->bal", readout_matrix, residual_row_block, preferred_element_type=jnp.float32
    )
    sample_outlook = sample_outlook.astype(jnp.bfloat16).reshape(
        sample_count, outlook_quantities, meridian_slab, zonal_points
    )
    row_index = (
        lax.axis_index("lat") * meridian_slab + jnp.arange(meridian_slab, dtype=jnp.int32)
    ).astype(jnp.float32)
    area = jnp.cos(math.pi * ((row_index + 0.5) / latitudes - 0.5))
    weight = (area * (1.0 / (latitudes * zonal_points)))[None, None, :, None]
    pair_norm = 1.0 / (ensemble * (ensemble - 1))
    owned_subset = sample_outlook.astype(jnp.float32)
    blank_buffer = jnp.zeros_like(owned_subset)
    spread, ranks = pair_terms(
        (blank_buffer, blank_buffer),
        owned_subset,
        lax.all_gather(sample_outlook, "ens", axis=0, tiled=True),
    )
    miss = owned_subset - observed_truth[None]
    loss_part = jnp.sum(weight * (smooth_magnitude(miss) / ensemble - 0.5 * pair_norm * spread))
    carried_signal = (weight * (smooth_slope(miss) / ensemble - pair_norm * ranks)).astype(
        jnp.bfloat16
    )
    carried_signal = carried_signal.reshape(sample_count, outlook_quantities, point_tally)
    sample_average_spread = spread / (ensemble - 1)
    readout_matrix_sensitivity = jnp.einsum(
        "mvp,mpc->vc", carried_signal, residual_row_block, preferred_element_type=jnp.float32
    )
    back_residual = jnp.einsum(
        "mvp,vc->mpc", carried_signal, readout_matrix, preferred_element_type=jnp.float32
    )
    back_residual = back_residual.astype(jnp.bfloat16).reshape(sample_count * point_tally, channels)
    shrink_matrix_sensitivity = lax.dot_general(
        nonlinear_response,
        back_residual,
        (((0,), (0,)), ((), ())),
        preferred_element_type=jnp.float32,
    )
    back_gate = lax.dot_general(
        back_residual, down_full, (((1,), (1,)), ((), ())), preferred_element_type=jnp.float32
    )
    back_upper = (back_gate * gelu_slope(northern_margin)).astype(jnp.bfloat16)
    widen_matrix_sensitivity = lax.dot_general(
        back_upper,
        standardized_activation,
        (((0,), (0,)), ((), ())),
        preferred_element_type=jnp.float32,
    )
    back_norm = jnp.dot(back_upper, up_full, preferred_element_type=jnp.float32).reshape(
        sample_count, meridian_slab, zonal_points, channels
    )
    affine_factor_sensitivity = jnp.sum(
        (back_norm * factor_multiplied).reshape(-1, channels), axis=0
    )
    back_scaled = back_norm * affine_factor
    back_depth = reciprocal_spread * (
        back_scaled
        - jnp.mean(back_scaled, axis=-1, keepdims=True)
        - factor_multiplied * jnp.mean(back_scaled * factor_multiplied, axis=-1, keepdims=True)
    )
    stencil_taps_sensitivity = kernel_grad(margin_extended, back_depth, meridian_slab)
    summed_up, summed_down = lax.psum((widen_matrix_sensitivity, shrink_matrix_sensitivity), "ens")
    owned_up, owned_down = (
        lax.psum_scatter(summed_up, "lat", scatter_dimension=0, tiled=True),
        lax.psum_scatter(summed_down, "lat", scatter_dimension=0, tiled=True),
    )
    crps_score, total_out, total_gain, total_kernel = lax.psum(
        (
            loss_part,
            readout_matrix_sensitivity,
            affine_factor_sensitivity,
            stencil_taps_sensitivity,
        ),
        ("ens", "lat"),
    )
    return (
        crps_score,
        total_kernel,
        total_gain,
        owned_up,
        owned_down,
        total_out,
        sample_outlook,
        sample_average_spread,
    )


def solution(mesh):
    in_specs = (
        P("lat", None, None),
        P("ens", "lat", None, None),
        P(None, "lat", None),
        P(),
        P(),
        P("lat", None),
        P("lat", None),
        P(),
    )
    out_specs = (
        P(),
        P(),
        P(),
        P("lat", None),
        P("lat", None),
        P(),
        P("ens", None, "lat", None),
        P("ens", None, "lat", None),
    )
    return jax.shard_map(
        on_device, mesh=mesh, in_specs=in_specs, out_specs=out_specs, check_vma=False
    )
```

profile of v0, /device:TPU:64, one launch (start us, length us, event | category | flops | bytes accessed | tf_op | source)
XLA Modules:
  0.0 579.8 jit_solution(15327835750314781220)
XLA Ops:
  7.2 1.0 fusion.8
  8.3 1.9 collective-permute-start
  10.2 3.6 collective-permute-start.1
  13.8 1.0 slice_bitcast_fusion.48
  14.9 1.0 slice_bitcast_fusion.47
  15.9 0.9 slice_bitcast_fusion.46
  16.8 53.0 %all_gather.9 = bf16[512,128]{1,0:T(8,128)(2,1)S(1)} all-gather(bf16[16,128]{1,0:T(8,128)(2,1)} %param.15), channel_id=1, replica_groups=mesh['ens'=16,'lat'=32] {'lat'}, dimensions={0}, use_global_device_ids=true | all-gather | bytes 135168 | tf_op jit(solution)/shard_map/all_gather | solution.py:132
  69.8 54.0 %all_gather.10 = bf16[512,128]{1,0:T(8,128)(2,1)S(1)} all-gather(bf16[16,128]{1,0:T(8,128)(2,1)} %param.16), channel_id=1, replica_groups=mesh['ens'=16,'lat'=32] {'lat'}, dimensions={0}, use_global_device_ids=true | all-gather | bytes 135168 | tf_op jit(solution)/shard_map/all_gather | solution.py:133
  125.3 1.1 maximum_convert_fusion.37
  126.4 1.3 maximum_convert_fusion.34
  128.9 0.6 maximum_convert_fusion.9
  131.7 3.9 fusion.14
  136.1 1.4 multiply_convert_fusion
  138.6 0.7 reshape.1579
  139.9 0.9 convert_element_type.102
  140.8 0.7 reshape.1584
  141.5 74.7 %all-gather.2.cloned.1.call-done = bf16[16,69,4,128]{3,2,1,0:T(4,128)(2,1)} async-done(((bf16[1,69,4,128]{3,2,1,0:T(4,128)(2,1)}), bf16[16,69,4,128]{3,2,1,0:T(4,128)(2,1)}) %all-gather.2.cloned.1.call-update) | async-done | bytes 1130512 | tf_op jit(solution)/shard_map/all_gather | solution.py:171
  216.3 17.6 %while.13 = (s32[]{:T(128)}, f32[1,69,4,128]{3,2,1,0:T(4,128)S(1)}, f32[1,69,4,128]{3,2,1,0:T(4,128)S(1)}, bf16[16,69,4,128]{3,2,1,0:T(4,128)(2,1)}, f32[1,69,4,128]{3,2,1,0:T(4,128)S(1)}, /*index=5*/s32[]{:T(128)}, s32[]{:T(128)}) while((s32[]{:T(128)}, f32[1,69,4,128]{3,2,1,0:T(4,128)S(1)}, f32[1,69,4,128]{3,2,1,0:T(4,128)S(1)}, ...), condition=%wide.region_3.4_spmd.clone, body=%wide.region_2.3_spmd.clone.sunk | while | flops 317955 | bytes 777307 | solution.py:107
  216.3 1.1 select_add_fusion.3
  217.4 1.1 select_add_fusion.3
  218.5 1.1 select_add_fusion.3
  219.6 1.1 select_add_fusion.3
  220.7 1.1 select_add_fusion.3
  221.8 1.1 select_add_fusion.3
  222.9 1.1 select_add_fusion.3
  224.0 1.1 select_add_fusion.3
  225.1 1.1 select_add_fusion.3
  226.2 1.1 select_add_fusion.3
  227.3 1.1 select_add_fusion.3
  228.4 1.1 select_add_fusion.3
  229.5 1.1 select_add_fusion.3
  230.6 1.1 select_add_fusion.3
  231.7 1.1 select_add_fusion.3
  232.8 1.1 select_add_fusion.3
  233.9 2.5 fusion.13
  236.7 1.1 fusion.21
  237.8 2.1 fusion
  240.3 0.7 multiply_reduce_fusion
  241.5 2.0 multiply_reduce_fusion.7
  243.5 1.8 multiply_reduce_fusion.17
  245.4 1.1 multiply_reduce_fusion.1
  246.6 1.8 multiply_reduce_fusion.28
  248.5 1.0 fusion.20
  249.8 1.1 multiply_reduce_fusion.38
  251.4 99.0 %all-reduce = (f32[]{:T(128)}, f32[49,128]{1,0:T(8,128)}, f32[128]{0:T(128)}, f32[69,128]{1,0:T(8,128)}) all-reduce(f32[]{:T(128)} %get-tuple-element.219, f32[49,128]{1,0:T(8,128)S(1)} %stack.199, f32[128]{0:T(128)S(1)} %copy-done.86, f32[69,128]{1,0:T(8,128)S(1)} %fusion.22), channel_id=1, replica_groups=mesh['ens'=16,'lat'=32] {'ens','lat'}, use_global_device_ids=true, to_apply=%region_5.6 | all-reduce | flops 15233 | bytes 121864 | tf_op jit(solution)/shard_map/psum | solution.py:221
  350.3 20.7 %reduce-scatter.5.cloned.1.call-done = f32[16,128]{1,0:T(8,128)} async-done(((f32[512,128]{1,0:T(8,128)}), f32[16,128]{1,0:T(8,128)}) %reduce-scatter.5.cloned.1.call-update) | async-done | bytes 8208 | tf_op jit(solution)/shard_map/reduce_scatter | solution.py:219
  371.0 125.0 %reduce-scatter.3.cloned.1.call-done = f32[16,128]{1,0:T(8,128)} async-done(((f32[512,128]{1,0:T(8,128)}), f32[16,128]{1,0:T(8,128)}) %reduce-scatter.3.cloned.1.call-update) | async-done | bytes 8208 | tf_op jit(solution)/shard_map/reduce_scatter | solution.py:218
  496.0 77.3 %all-reduce.1 = (f32[16,128]{1,0:T(8,128)}, f32[16,128]{1,0:T(8,128)}) all-reduce(f32[16,128]{1,0:T(8,128)} %reduce-scatter.3.cloned.1.call-done, f32[16,128]{1,0:T(8,128)} %reduce-scatter.5.cloned.1.call-done), channel_id=1, replica_groups=mesh['ens'=16,'lat'=32] {'ens'}, use_global_device_ids=true, to_apply=%region_60.61 | all-reduce | flops 4096 | bytes 32768 | tf_op jit(solution)/shard_map/psum | solution.py:216
  (249 shorter events, 8.0 us)
Async XLA Ops:
  7.2 131.2 %copy-start = (bf16[69,128]{1,0:T(8,128)(2,1)S(1)}, bf16[69,128]{1,0:T(8,128)(2,1)}, u32[]{:S(2)}) copy-start(bf16[69,128]{1,0:T(8,128)(2,1)} %param.17) | copy-start | bytes 52996
  7.2 209.1 %all-gather.2.cloned.1.call-start = ((), (), s32[]{:S(2)}) async-start(), calls=%async_computation.2 | async-start | bytes 1201152 | tf_op jit(solution)/shard_map/all_gather | solution.py:171
  8.3 115.6 %collective-permute-start = (bf16[1,3,128,128]{3,2,1,0:T(8,128)(2,1)S(1)}, bf16[1,3,128,128]{3,2,1,0:T(8,128)(2,1)S(1)}, u32[]{:S(2)}, u32[]{:S(2)}) collective-permute-start(bf16[1,3,128,128]{3,2,1,0:T(8,128)(2,1)S(1)} %get-tuple-element.221), channel_id=1, source_target_pairs={{0,1},{1,2},{2,3},{3,4},{4,5},{5,6},{6,7},{7,8},{8,9},{9,10},{10,1... | collective-permute-start | bytes 294920 | tf_op jit(solution)/shard_map/ppermute | solution.py:22
  10.2 113.7 %collective-permute-start.1 = (bf16[1,3,128,128]{3,2,1,0:T(8,128)(2,1)S(1)}, bf16[1,3,128,128]{3,2,1,0:T(8,128)(2,1)S(1)}, u32[]{:S(2)}, u32[]{:S(2)}) collective-permute-start(bf16[1,3,128,128]{3,2,1,0:T(8,128)(2,1)S(1)} %get-tuple-element.222), channel_id=1, source_target_pairs={{1,0},{2,1},{3,2},{4,3},{5,4},{6,5},{7,6},{8,7},{9,8},{10,9},{11,1... | collective-permute-start | bytes 294920 | tf_op jit(solution)/shard_map/ppermute | solution.py:24
  69.8 66.3 %copy-start.68 = (bf16[512,128]{1,0:T(8,128)(2,1)}, bf16[512,128]{1,0:T(8,128)(2,1)S(1)}, u32[]{:S(2)}) copy-start(bf16[512,128]{1,0:T(8,128)(2,1)S(1)} %all_gather.9) | copy-start | bytes 393220
  123.8 13.7 %copy-start.70 = (bf16[512,128]{1,0:T(8,128)(2,1)}, bf16[512,128]{1,0:T(8,128)(2,1)S(1)}, u32[]{:S(2)}) copy-start(bf16[512,128]{1,0:T(8,128)(2,1)S(1)} %all_gather.10) | copy-start | bytes 393220
  124.2 7.1 %copy-start.7 = (f32[1,4,125,128]{3,2,1,0:T(8,128)}, f32[1,4,125,128]{3,2,1,0:T(8,128)S(1)}, u32[]{:S(2)}) copy-start(f32[1,4,125,128]{3,2,1,0:T(8,128)S(1)} %get-tuple-element.141) | copy-start | bytes 768004
  124.2 7.1 %copy-start.9 = (f32[1,4,125,128]{3,2,1,0:T(8,128)}, f32[1,4,125,128]{3,2,1,0:T(8,128)S(1)}, u32[]{:S(2)}) copy-start(f32[1,4,125,128]{3,2,1,0:T(8,128)S(1)} %get-tuple-element.142) | copy-start | bytes 768004
  124.2 7.1 %copy-start.11 = (f32[1,4,125,128]{3,2,1,0:T(8,128)}, f32[1,4,125,128]{3,2,1,0:T(8,128)S(1)}, u32[]{:S(2)}) copy-start(f32[1,4,125,128]{3,2,1,0:T(8,128)S(1)} %get-tuple-element.145) | copy-start | bytes 768004
  124.3 7.1 %copy-start.12 = (f32[1,4,125,128]{3,2,1,0:T(8,128)}, f32[1,4,125,128]{3,2,1,0:T(8,128)S(1)}, u32[]{:S(2)}) copy-start(f32[1,4,125,128]{3,2,1,0:T(8,128)S(1)} %get-tuple-element.146) | copy-start | bytes 768004
  124.3 7.1 %copy-start.18 = (f32[1,4,125,128]{3,2,1,0:T(8,128)}, f32[1,4,125,128]{3,2,1,0:T(8,128)S(1)}, u32[]{:S(2)}) copy-start(f32[1,4,125,128]{3,2,1,0:T(8,128)S(1)} %get-tuple-element.152) | copy-start | bytes 768004
  124.3 7.1 %copy-start.28 = (f32[1,4,125,128]{3,2,1,0:T(8,128)}, f32[1,4,125,128]{3,2,1,0:T(8,128)S(1)}, u32[]{:S(2)}) copy-start(f32[1,4,125,128]{3,2,1,0:T(8,128)S(1)} %get-tuple-element.147) | copy-start | bytes 768004
  124.3 7.1 %copy-start.44 = (f32[1,4,125,128]{3,2,1,0:T(8,128)}, f32[1,4,125,128]{3,2,1,0:T(8,128)S(1)}, u32[]{:S(2)}) copy-start(f32[1,4,125,128]{3,2,1,0:T(8,128)S(1)} %get-tuple-element.140) | copy-start | bytes 768004
  124.3 7.1 %copy-start.46 = (f32[1,4,125,128]{3,2,1,0:T(8,128)}, f32[1,4,125,128]{3,2,1,0:T(8,128)S(1)}, u32[]{:S(2)}) copy-start(f32[1,4,125,128]{3,2,1,0:T(8,128)S(1)} %get-tuple-element.143) | copy-start | bytes 768004
  124.3 7.1 %copy-start.48 = (f32[1,4,125,128]{3,2,1,0:T(8,128)}, f32[1,4,125,128]{3,2,1,0:T(8,128)S(1)}, u32[]{:S(2)}) copy-start(f32[1,4,125,128]{3,2,1,0:T(8,128)S(1)} %get-tuple-element.148) | copy-start | bytes 768004
  124.3 7.1 %copy-start.50 = (f32[1,4,125,128]{3,2,1,0:T(8,128)}, f32[1,4,125,128]{3,2,1,0:T(8,128)S(1)}, u32[]{:S(2)}) copy-start(f32[1,4,125,128]{3,2,1,0:T(8,128)S(1)} %get-tuple-element.151) | copy-start | bytes 768004
  124.6 6.8 %copy-start.13 = (f32[1,4,126,128]{3,2,1,0:T(8,128)}, f32[1,4,126,128]{3,2,1,0:T(8,128)S(1)}, u32[]{:S(2)}) copy-start(f32[1,4,126,128]{3,2,1,0:T(8,128)S(1)} %get-tuple-element.159) | copy-start | bytes 774148
  124.6 6.8 %copy-start.14 = (f32[1,4,126,128]{3,2,1,0:T(8,128)}, f32[1,4,126,128]{3,2,1,0:T(8,128)S(1)}, u32[]{:S(2)}) copy-start(f32[1,4,126,128]{3,2,1,0:T(8,128)S(1)} %get-tuple-element.161) | copy-start | bytes 774148
  124.7 6.8 %copy-start.15 = (f32[1,4,126,128]{3,2,1,0:T(8,128)}, f32[1,4,126,128]{3,2,1,0:T(8,128)S(1)}, u32[]{:S(2)}) copy-start(f32[1,4,126,128]{3,2,1,0:T(8,128)S(1)} %get-tuple-element.162) | copy-start | bytes 774148
  124.7 6.8 %copy-start.20 = (f32[1,4,126,128]{3,2,1,0:T(8,128)}, f32[1,4,126,128]{3,2,1,0:T(8,128)S(1)}, u32[]{:S(2)}) copy-start(f32[1,4,126,128]{3,2,1,0:T(8,128)S(1)} %get-tuple-element.160) | copy-start | bytes 774148
  124.7 6.8 %copy-start.22 = (f32[1,4,126,128]{3,2,1,0:T(8,128)}, f32[1,4,126,128]{3,2,1,0:T(8,128)S(1)}, u32[]{:S(2)}) copy-start(f32[1,4,126,128]{3,2,1,0:T(8,128)S(1)} %get-tuple-element.164) | copy-start | bytes 774148
  124.7 6.8 %copy-start.30 = (f32[1,4,126,128]{3,2,1,0:T(8,128)}, f32[1,4,126,128]{3,2,1,0:T(8,128)S(1)}, u32[]{:S(2)}) copy-start(f32[1,4,126,128]{3,2,1,0:T(8,128)S(1)} %get-tuple-element.154) | copy-start | bytes 774148
  124.7 6.8 %copy-start.32 = (f32[1,4,126,128]{3,2,1,0:T(8,128)}, f32[1,4,126,128]{3,2,1,0:T(8,128)S(1)}, u32[]{:S(2)}) copy-start(f32[1,4,126,128]{3,2,1,0:T(8,128)S(1)} %get-tuple-element.157) | copy-start | bytes 774148
  124.7 6.8 %copy-start.34 = (f32[1,4,126,128]{3,2,1,0:T(8,128)}, f32[1,4,126,128]{3,2,1,0:T(8,128)S(1)}, u32[]{:S(2)}) copy-start(f32[1,4,126,128]{3,2,1,0:T(8,128)S(1)} %get-tuple-element.166) | copy-start | bytes 774148
  124.7 6.8 %copy-start.52 = (f32[1,4,126,128]{3,2,1,0:T(8,128)}, f32[1,4,126,128]{3,2,1,0:T(8,128)S(1)}, u32[]{:S(2)}) copy-start(f32[1,4,126,128]{3,2,1,0:T(8,128)S(1)} %get-tuple-element.155) | copy-start | bytes 774148
  124.7 6.8 %copy-start.54 = (f32[1,4,126,128]{3,2,1,0:T(8,128)}, f32[1,4,126,128]{3,2,1,0:T(8,128)S(1)}, u32[]{:S(2)}) copy-start(f32[1,4,126,128]{3,2,1,0:T(8,128)S(1)} %get-tuple-element.156) | copy-start | bytes 774148
  124.7 6.8 %copy-start.56 = (f32[1,4,126,128]{3,2,1,0:T(8,128)}, f32[1,4,126,128]{3,2,1,0:T(8,128)S(1)}, u32[]{:S(2)}) copy-start(f32[1,4,126,128]{3,2,1,0:T(8,128)S(1)} %get-tuple-element.158) | copy-start | bytes 774148
  125.1 6.4 %copy-start.1 = (f32[1,4,127,128]{3,2,1,0:T(8,128)}, f32[1,4,127,128]{3,2,1,0:T(8,128)S(1)}, u32[]{:S(2)}) copy-start(f32[1,4,127,128]{3,2,1,0:T(8,128)S(1)} %get-tuple-element.176) | copy-start | bytes 780292
  125.1 6.4 %copy-start.3 = (f32[1,4,127,128]{3,2,1,0:T(8,128)}, f32[1,4,127,128]{3,2,1,0:T(8,128)S(1)}, u32[]{:S(2)}) copy-start(f32[1,4,127,128]{3,2,1,0:T(8,128)S(1)} %get-tuple-element.177) | copy-start | bytes 780292
  125.1 6.4 %copy-start.5 = (f32[1,4,127,128]{3,2,1,0:T(8,128)}, f32[1,4,127,128]{3,2,1,0:T(8,128)S(1)}, u32[]{:S(2)}) copy-start(f32[1,4,127,128]{3,2,1,0:T(8,128)S(1)} %get-tuple-element.179) | copy-start | bytes 780292
  125.1 6.4 %copy-start.16 = (f32[1,4,127,128]{3,2,1,0:T(8,128)}, f32[1,4,127,128]{3,2,1,0:T(8,128)S(1)}, u32[]{:S(2)}) copy-start(f32[1,4,127,128]{3,2,1,0:T(8,128)S(1)} %get-tuple-element.171) | copy-start | bytes 780292
  125.1 6.4 %copy-start.17 = (f32[1,4,127,128]{3,2,1,0:T(8,128)}, f32[1,4,127,128]{3,2,1,0:T(8,128)S(1)}, u32[]{:S(2)}) copy-start(f32[1,4,127,128]{3,2,1,0:T(8,128)S(1)} %get-tuple-element.173) | copy-start | bytes 780292
  125.1 6.4 %copy-start.24 = (f32[1,4,127,128]{3,2,1,0:T(8,128)}, f32[1,4,127,128]{3,2,1,0:T(8,128)S(1)}, u32[]{:S(2)}) copy-start(f32[1,4,127,128]{3,2,1,0:T(8,128)S(1)} %get-tuple-element.175) | copy-start | bytes 780292
  125.2 6.4 %copy-start.26 = (f32[1,4,127,128]{3,2,1,0:T(8,128)}, f32[1,4,127,128]{3,2,1,0:T(8,128)S(1)}, u32[]{:S(2)}) copy-start(f32[1,4,127,128]{3,2,1,0:T(8,128)S(1)} %get-tuple-element.178) | copy-start | bytes 780292
  125.2 6.4 %copy-start.36 = (f32[1,4,127,128]{3,2,1,0:T(8,128)}, f32[1,4,127,128]{3,2,1,0:T(8,128)S(1)}, u32[]{:S(2)}) copy-start(f32[1,4,127,128]{3,2,1,0:T(8,128)S(1)} %get-tuple-element.168) | copy-start | bytes 780292
  125.2 6.4 %copy-start.38 = (f32[1,4,127,128]{3,2,1,0:T(8,128)}, f32[1,4,127,128]{3,2,1,0:T(8,128)S(1)}, u32[]{:S(2)}) copy-start(f32[1,4,127,128]{3,2,1,0:T(8,128)S(1)} %get-tuple-element.169) | copy-start | bytes 780292
  125.2 6.4 %copy-start.40 = (f32[1,4,127,128]{3,2,1,0:T(8,128)}, f32[1,4,127,128]{3,2,1,0:T(8,128)S(1)}, u32[]{:S(2)}) copy-start(f32[1,4,127,128]{3,2,1,0:T(8,128)S(1)} %get-tuple-element.170) | copy-start | bytes 780292
  125.2 6.4 %copy-start.42 = (f32[1,4,127,128]{3,2,1,0:T(8,128)}, f32[1,4,127,128]{3,2,1,0:T(8,128)S(1)}, u32[]{:S(2)}) copy-start(f32[1,4,127,128]{3,2,1,0:T(8,128)S(1)} %get-tuple-element.174) | copy-start | bytes 780292
  125.2 10.4 %copy-start.58 = (f32[1,4,127,128]{3,2,1,0:T(8,128)}, f32[1,4,127,128]{3,2,1,0:T(8,128)S(1)}, u32[]{:S(2)}) copy-start(f32[1,4,127,128]{3,2,1,0:T(8,128)S(1)} %get-tuple-element.172) | copy-start | bytes 780292
  125.2 10.4 %copy-start.60 = (f32[1,4,127,128]{3,2,1,0:T(8,128)}, f32[1,4,127,128]{3,2,1,0:T(8,128)S(1)}, u32[]{:S(2)}) copy-start(f32[1,4,127,128]{3,2,1,0:T(8,128)S(1)} %get-tuple-element.180) | copy-start | bytes 780292
  125.2 10.3 %copy-start.74 = (f32[1,4,3,128]{3,2,1,0:T(4,128)}, f32[1,4,3,128]{3,2,1,0:T(4,128)S(1)}, u32[]{:S(2)}) copy-start(f32[1,4,3,128]{3,2,1,0:T(4,128)S(1)} %get-tuple-element.134) | copy-start | bytes 18436
  125.3 10.3 %copy-start.76 = (f32[1,4,3,128]{3,2,1,0:T(4,128)}, f32[1,4,3,128]{3,2,1,0:T(4,128)S(1)}, u32[]{:S(2)}) copy-start(f32[1,4,3,128]{3,2,1,0:T(4,128)S(1)} %get-tuple-element.135) | copy-start | bytes 18436
  125.3 10.3 %copy-start.78 = (f32[1,4,3,128]{3,2,1,0:T(4,128)}, f32[1,4,3,128]{3,2,1,0:T(4,128)S(1)}, u32[]{:S(2)}) copy-start(f32[1,4,3,128]{3,2,1,0:T(4,128)S(1)} %get-tuple-element.136) | copy-start | bytes 18436
  131.7 4.2 copy-start.84
  139.3 231.7 %reduce-scatter.5.cloned.1.call-start = ((), (), s32[]{:S(2)}) async-start(), calls=%async_computation.4 | async-start | bytes 270336 | tf_op jit(solution)/shard_map/reduce_scatter | solution.py:219
  216.3 17.6 %copy-start.105 = (f32[4]{0:T(128)S(1)}, f32[4]{0:T(128)}, u32[]{:S(2)}) copy-start(f32[4]{0:T(128)} %cosine_multiply_fusion) | copy-start | bytes 52
  233.9 3.9 copy-start.71
  246.5 249.5 %reduce-scatter.3.cloned.1.call-start = ((), (), s32[]{:S(2)}) async-start(), calls=%async_computation.3 | async-start | bytes 270336 | tf_op jit(solution)/shard_map/reduce_scatter | solution.py:218
  (63 other events, 103.6 us)
Sparse Core Ops, SparseCore 0:
  139.4 76.8 all-gather.1
  246.6 124.4 reduce-scatter.4
  375.6 120.3 reduce-scatter.2
where the time goes:
time: 581 us; the launch traced here: 580 us
  blocking collectives  283 us (49%)
  waiting for transfers between devices  220 us (38%)
  other arithmetic  41.3 us (7%)
  between operations  15.3 us (3%)
  matrix products  6.82 us (1%)
  local copies, waits for them, and re-layouts  6.71 us (1%)
    reduce_scatter x1, waiting for transfers between devices, on_device(): lax.psum_scatter(summed_up, 'lat', scatter_dimension=0, tiled=True)  125 us
    psum x1, blocking collectives, on_device(): lax.psum((loss_part, readout_matrix_sensitivity, affine_factor_sensitivit...  99 us
    psum x1, blocking collectives, on_device(): lax.psum((widen_matrix_sensitivity, shrink_matrix_sensitivity), 'ens')  77.3 us
    all_gather x1, waiting for transfers between devices, on_device(): lax.all_gather(sample_outlook, 'ens', axis=0, tiled=True)  74.7 us
    all_gather x1, blocking collectives, on_device(): lax.all_gather(shrink_matrix, 'lat', axis=0, tiled=True)  54 us
    all_gather x1, blocking collectives, on_device(): lax.all_gather(widen_matrix, 'lat', axis=0, tiled=True)  53 us
    reduce_scatter x1, waiting for transfers between devices, on_device(): lax.psum_scatter(summed_down, 'lat', scatter_dimension=0, tiled=True)  20.7 us
    add x16, other arithmetic, one_pair(): totals[1] + smooth_slope(gap)  17.3 us
  transfers between devices with their start and end apart: 5, of which 3 were waited for; matrix products, arithmetic and copies ran while one was open for 2% of the time, Pallas kernels for 0%

commit v1 on v0

--- a/solution.py
+++ b/solution.py
@@ -168,7 +168,9 @@
     spread, ranks = pair_terms(
         (blank_buffer, blank_buffer),
         owned_subset,
-        lax.all_gather(sample_outlook, "ens", axis=0, tiled=True),
+        jnp.concatenate(
+            lax.all_to_all(jnp.stack([sample_outlook] * lax.axis_size("ens")), "ens", 0, 0), axis=0
+        ),
     )
     miss = owned_subset - observed_truth[None]
     loss_part = jnp.sum(weight * (smooth_magnitude(miss) / ensemble - 0.5 * pair_norm * spread))

time: 581 us -> 532 us (0.916)
  waiting for transfers between devices: 220 us -> 172 us
  blocking collectives: 283 us -> 277 us
    all_gather x1 -> x0, waiting for transfers between devices: 74.7 us -> none  [on_device(): lax.all_gather(sample_outlook, 'ens', axis=0, tiled=True)]
    all_to_all x0 -> x1, waiting for transfers between devices: none -> 27.9 us  [on_device(): lax.all_to_all(jnp.stack([sample_outlook] * lax.axis_size('ens')), 'ens',...]
where the time goes in v1:
time: 532 us; the launch traced here: 531 us
  blocking collectives  277 us (52%)
  waiting for transfers between devices  172 us (32%)
  other arithmetic  41.1 us (8%)
  between operations  15.6 us (3%)
  starting transfers between devices  10.4 us (2%)
  local copies, waits for them, and re-layouts  7.39 us (1%)
  matrix products  6.79 us (1%)
    reduce_scatter x1, waiting for transfers between devices, on_device(): lax.psum_scatter(summed_up, 'lat', scatter_dimension=0, tiled=True)  125 us
    psum x1, blocking collectives, on_device(): lax.psum((loss_part, readout_matrix_sensitivity, affine_factor_sensitivit...  93.3 us
    psum x1, blocking collectives, on_device(): lax.psum((widen_matrix_sensitivity, shrink_matrix_sensitivity), 'ens')  77.1 us
    all_gather x1, blocking collectives, on_device(): lax.all_gather(shrink_matrix, 'lat', axis=0, tiled=True)  54 us
    all_gather x1, blocking collectives, on_device(): lax.all_gather(widen_matrix, 'lat', axis=0, tiled=True)  53 us
    all_to_all x1, waiting for transfers between devices, on_device(): lax.all_to_all(jnp.stack([sample_outlook] * lax.axis_size('ens')), 'ens',...  27.9 us
    reduce_scatter x1, waiting for transfers between devices, on_device(): lax.psum_scatter(summed_down, 'lat', scatter_dimension=0, tiled=True)  18.9 us
    add x16, other arithmetic, one_pair(): totals[1] + smooth_slope(gap)  17.3 us
  transfers between devices with their start and end apart: 5, of which 3 were waited for; matrix products, arithmetic and copies ran while one was open for 2% of the time, Pallas kernels for 0%

profile of v1, /device:TPU:64, one launch (start us, length us, event | category | flops | bytes accessed | tf_op | source)
XLA Modules:
  0.0 530.9 jit_solution(11647371463843942749)
XLA Ops:
  7.2 1.0 fusion.8
  8.2 1.9 collective-permute-start
  10.2 3.6 collective-permute-start.1
  13.8 1.0 slice_bitcast_fusion.48
  14.8 1.0 slice_bitcast_fusion.47
  15.8 0.9 slice_bitcast_fusion.46
  16.7 53.0 %all_gather.6 = bf16[512,128]{1,0:T(8,128)(2,1)S(1)} all-gather(bf16[16,128]{1,0:T(8,128)(2,1)} %param.15), channel_id=1, replica_groups=mesh['ens'=16,'lat'=32] {'lat'}, dimensions={0}, use_global_device_ids=true | all-gather | bytes 135168 | tf_op jit(solution)/shard_map/all_gather | solution.py:132
  69.8 54.0 %all_gather.7 = bf16[512,128]{1,0:T(8,128)(2,1)S(1)} all-gather(bf16[16,128]{1,0:T(8,128)(2,1)} %param.16), channel_id=1, replica_groups=mesh['ens'=16,'lat'=32] {'lat'}, dimensions={0}, use_global_device_ids=true | all-gather | bytes 135168 | tf_op jit(solution)/shard_map/all_gather | solution.py:133
  125.2 1.1 maximum_convert_fusion.37
  126.3 1.2 maximum_convert_fusion.34
  131.5 3.9 fusion.14
  135.9 1.4 multiply_convert_fusion
  138.4 1.3 stack.153
  139.7 4.8 all-to-all-start
  145.2 0.7 reshape.1588
  145.8 0.9 convert_element_type.98
  146.7 27.9 %all-to-all-done = bf16[16,1,69,4,128]{4,3,2,1,0:T(4,128)(2,1)} async-done(((bf16[16,1,69,4,128]{4,3,2,1,0:T(4,128)(2,1)}), bf16[16,1,69,4,128]{4,3,2,1,0:T(4,128)(2,1)}, u32[]{:S(2)}, u32[]{:S(2)}) %all-to-all-start) | async-done | bytes 1130528 | tf_op jit(solution)/shard_map/all_to_all | solution.py:172
  174.6 17.5 %while.13 = (s32[]{:T(128)}, f32[1,69,4,128]{3,2,1,0:T(4,128)S(1)}, f32[1,69,4,128]{3,2,1,0:T(4,128)S(1)}, bf16[16,69,4,128]{3,2,1,0:T(4,128)(2,1)}, f32[1,69,4,128]{3,2,1,0:T(4,128)S(1)}, /*index=5*/s32[]{:T(128)}, s32[]{:T(128)}) while((s32[]{:T(128)}, f32[1,69,4,128]{3,2,1,0:T(4,128)S(1)}, f32[1,69,4,128]{3,2,1,0:T(4,128)S(1)}, ...), condition=%wide.region_3.4_spmd.clone, body=%wide.region_2.3_spmd.clone.sunk | while | flops 317955 | bytes 777307 | solution.py:107
  174.6 1.1 select_add_fusion.3
  175.7 1.1 select_add_fusion.3
  176.8 1.1 select_add_fusion.3
  177.9 1.1 select_add_fusion.3
  179.0 1.1 select_add_fusion.3
  180.1 1.1 select_add_fusion.3
  181.2 1.1 select_add_fusion.3
  182.3 1.1 select_add_fusion.3
  183.4 1.1 select_add_fusion.3
  184.5 1.1 select_add_fusion.3
  185.6 1.1 select_add_fusion.3
  186.7 1.1 select_add_fusion.3
  187.8 1.1 select_add_fusion.3
  188.9 1.1 select_add_fusion.3
  190.0 1.1 select_add_fusion.3
  191.1 1.1 select_add_fusion.3
  192.2 2.5 fusion.13
  195.0 1.0 fusion.21
  196.1 2.1 fusion
  198.7 0.7 multiply_reduce_fusion
  199.8 2.0 multiply_reduce_fusion.7
  201.9 1.7 multiply_reduce_fusion.17
  203.7 1.1 multiply_reduce_fusion.1
  204.9 1.8 multiply_reduce_fusion.28
  206.9 1.0 fusion.20
  208.1 1.1 multiply_reduce_fusion.38
  209.7 93.3 %all-reduce = (f32[]{:T(128)}, f32[49,128]{1,0:T(8,128)}, f32[128]{0:T(128)}, f32[69,128]{1,0:T(8,128)}) all-reduce(f32[]{:T(128)} %get-tuple-element.219, f32[49,128]{1,0:T(8,128)S(1)} %stack.203, f32[128]{0:T(128)S(1)} %copy-done.86, f32[69,128]{1,0:T(8,128)S(1)} %fusion.22), channel_id=1, replica_groups=mesh['ens'=16,'lat'=32] {'ens','lat'}, use_global_device_ids=true, to_apply=%region_5.6 | all-reduce | flops 15233 | bytes 121864 | tf_op jit(solution)/shard_map/psum | solution.py:223
  303.0 18.9 %reduce-scatter.5.cloned.1.call-done = f32[16,128]{1,0:T(8,128)} async-done(((f32[512,128]{1,0:T(8,128)}), f32[16,128]{1,0:T(8,128)}) %reduce-scatter.5.cloned.1.call-update) | async-done | bytes 8208 | tf_op jit(solution)/shard_map/reduce_scatter | solution.py:221
  321.9 125.0 %reduce-scatter.3.cloned.1.call-done = f32[16,128]{1,0:T(8,128)} async-done(((f32[512,128]{1,0:T(8,128)}), f32[16,128]{1,0:T(8,128)}) %reduce-scatter.3.cloned.1.call-update) | async-done | bytes 8208 | tf_op jit(solution)/shard_map/reduce_scatter | solution.py:220
  446.9 77.1 %all-reduce.1 = (f32[16,128]{1,0:T(8,128)}, f32[16,128]{1,0:T(8,128)}) all-reduce(f32[16,128]{1,0:T(8,128)} %reduce-scatter.3.cloned.1.call-done, f32[16,128]{1,0:T(8,128)} %reduce-scatter.5.cloned.1.call-done), channel_id=1, replica_groups=mesh['ens'=16,'lat'=32] {'ens'}, use_global_device_ids=true, to_apply=%region_60.61 | all-reduce | flops 4096 | bytes 32768 | tf_op jit(solution)/shard_map/psum | solution.py:218
  (247 shorter events, 8.6 us)
Async XLA Ops:
  7.2 131.0 %copy-start = (bf16[69,128]{1,0:T(8,128)(2,1)S(1)}, bf16[69,128]{1,0:T(8,128)(2,1)}, u32[]{:S(2)}) copy-start(bf16[69,128]{1,0:T(8,128)(2,1)} %param.17) | copy-start | bytes 52996
  8.2 115.6 %collective-permute-start = (bf16[1,3,128,128]{3,2,1,0:T(8,128)(2,1)S(1)}, bf16[1,3,128,128]{3,2,1,0:T(8,128)(2,1)S(1)}, u32[]{:S(2)}, u32[]{:S(2)}) collective-permute-start(bf16[1,3,128,128]{3,2,1,0:T(8,128)(2,1)S(1)} %get-tuple-element.221), channel_id=1, source_target_pairs={{0,1},{1,2},{2,3},{3,4},{4,5},{5,6},{6,7},{7,8},{8,9},{9,10},{10,1... | collective-permute-start | bytes 294920 | tf_op jit(solution)/shard_map/ppermute | solution.py:22
  10.2 113.7 %collective-permute-start.1 = (bf16[1,3,128,128]{3,2,1,0:T(8,128)(2,1)S(1)}, bf16[1,3,128,128]{3,2,1,0:T(8,128)(2,1)S(1)}, u32[]{:S(2)}, u32[]{:S(2)}) collective-permute-start(bf16[1,3,128,128]{3,2,1,0:T(8,128)(2,1)S(1)} %get-tuple-element.222), channel_id=1, source_target_pairs={{1,0},{2,1},{3,2},{4,3},{5,4},{6,5},{7,6},{8,7},{9,8},{10,9},{11,1... | collective-permute-start | bytes 294920 | tf_op jit(solution)/shard_map/ppermute | solution.py:24
  69.8 66.2 %copy-start.68 = (bf16[512,128]{1,0:T(8,128)(2,1)}, bf16[512,128]{1,0:T(8,128)(2,1)S(1)}, u32[]{:S(2)}) copy-start(bf16[512,128]{1,0:T(8,128)(2,1)S(1)} %all_gather.6) | copy-start | bytes 393220
  123.8 13.5 %copy-start.70 = (bf16[512,128]{1,0:T(8,128)(2,1)}, bf16[512,128]{1,0:T(8,128)(2,1)S(1)}, u32[]{:S(2)}) copy-start(bf16[512,128]{1,0:T(8,128)(2,1)S(1)} %all_gather.7) | copy-start | bytes 393220
  124.2 7.0 %copy-start.7 = (f32[1,4,125,128]{3,2,1,0:T(8,128)}, f32[1,4,125,128]{3,2,1,0:T(8,128)S(1)}, u32[]{:S(2)}) copy-start(f32[1,4,125,128]{3,2,1,0:T(8,128)S(1)} %get-tuple-element.141) | copy-start | bytes 768004
  124.2 7.0 %copy-start.9 = (f32[1,4,125,128]{3,2,1,0:T(8,128)}, f32[1,4,125,128]{3,2,1,0:T(8,128)S(1)}, u32[]{:S(2)}) copy-start(f32[1,4,125,128]{3,2,1,0:T(8,128)S(1)} %get-tuple-element.142) | copy-start | bytes 768004
  124.2 6.9 %copy-start.11 = (f32[1,4,125,128]{3,2,1,0:T(8,128)}, f32[1,4,125,128]{3,2,1,0:T(8,128)S(1)}, u32[]{:S(2)}) copy-start(f32[1,4,125,128]{3,2,1,0:T(8,128)S(1)} %get-tuple-element.145) | copy-start | bytes 768004
  124.2 6.9 %copy-start.12 = (f32[1,4,125,128]{3,2,1,0:T(8,128)}, f32[1,4,125,128]{3,2,1,0:T(8,128)S(1)}, u32[]{:S(2)}) copy-start(f32[1,4,125,128]{3,2,1,0:T(8,128)S(1)} %get-tuple-element.146) | copy-start | bytes 768004
  124.2 6.9 %copy-start.18 = (f32[1,4,125,128]{3,2,1,0:T(8,128)}, f32[1,4,125,128]{3,2,1,0:T(8,128)S(1)}, u32[]{:S(2)}) copy-start(f32[1,4,125,128]{3,2,1,0:T(8,128)S(1)} %get-tuple-element.152) | copy-start | bytes 768004
  124.2 6.9 %copy-start.28 = (f32[1,4,125,128]{3,2,1,0:T(8,128)}, f32[1,4,125,128]{3,2,1,0:T(8,128)S(1)}, u32[]{:S(2)}) copy-start(f32[1,4,125,128]{3,2,1,0:T(8,128)S(1)} %get-tuple-element.147) | copy-start | bytes 768004
  124.2 6.9 %copy-start.44 = (f32[1,4,125,128]{3,2,1,0:T(8,128)}, f32[1,4,125,128]{3,2,1,0:T(8,128)S(1)}, u32[]{:S(2)}) copy-start(f32[1,4,125,128]{3,2,1,0:T(8,128)S(1)} %get-tuple-element.140) | copy-start | bytes 768004
  124.2 6.9 %copy-start.46 = (f32[1,4,125,128]{3,2,1,0:T(8,128)}, f32[1,4,125,128]{3,2,1,0:T(8,128)S(1)}, u32[]{:S(2)}) copy-start(f32[1,4,125,128]{3,2,1,0:T(8,128)S(1)} %get-tuple-element.143) | copy-start | bytes 768004
  124.3 6.9 %copy-start.48 = (f32[1,4,125,128]{3,2,1,0:T(8,128)}, f32[1,4,125,128]{3,2,1,0:T(8,128)S(1)}, u32[]{:S(2)}) copy-start(f32[1,4,125,128]{3,2,1,0:T(8,128)S(1)} %get-tuple-element.148) | copy-start | bytes 768004
  124.3 6.9 %copy-start.50 = (f32[1,4,125,128]{3,2,1,0:T(8,128)}, f32[1,4,125,128]{3,2,1,0:T(8,128)S(1)}, u32[]{:S(2)}) copy-start(f32[1,4,125,128]{3,2,1,0:T(8,128)S(1)} %get-tuple-element.151) | copy-start | bytes 768004
  124.6 6.6 %copy-start.13 = (f32[1,4,126,128]{3,2,1,0:T(8,128)}, f32[1,4,126,128]{3,2,1,0:T(8,128)S(1)}, u32[]{:S(2)}) copy-start(f32[1,4,126,128]{3,2,1,0:T(8,128)S(1)} %get-tuple-element.159) | copy-start | bytes 774148
  124.6 6.6 %copy-start.14 = (f32[1,4,126,128]{3,2,1,0:T(8,128)}, f32[1,4,126,128]{3,2,1,0:T(8,128)S(1)}, u32[]{:S(2)}) copy-start(f32[1,4,126,128]{3,2,1,0:T(8,128)S(1)} %get-tuple-element.161) | copy-start | bytes 774148
  124.6 6.6 %copy-start.15 = (f32[1,4,126,128]{3,2,1,0:T(8,128)}, f32[1,4,126,128]{3,2,1,0:T(8,128)S(1)}, u32[]{:S(2)}) copy-start(f32[1,4,126,128]{3,2,1,0:T(8,128)S(1)} %get-tuple-element.162) | copy-start | bytes 774148
  124.6 6.6 %copy-start.20 = (f32[1,4,126,128]{3,2,1,0:T(8,128)}, f32[1,4,126,128]{3,2,1,0:T(8,128)S(1)}, u32[]{:S(2)}) copy-start(f32[1,4,126,128]{3,2,1,0:T(8,128)S(1)} %get-tuple-element.160) | copy-start | bytes 774148
  124.6 6.6 %copy-start.22 = (f32[1,4,126,128]{3,2,1,0:T(8,128)}, f32[1,4,126,128]{3,2,1,0:T(8,128)S(1)}, u32[]{:S(2)}) copy-start(f32[1,4,126,128]{3,2,1,0:T(8,128)S(1)} %get-tuple-element.164) | copy-start | bytes 774148
  124.6 6.6 %copy-start.30 = (f32[1,4,126,128]{3,2,1,0:T(8,128)}, f32[1,4,126,128]{3,2,1,0:T(8,128)S(1)}, u32[]{:S(2)}) copy-start(f32[1,4,126,128]{3,2,1,0:T(8,128)S(1)} %get-tuple-element.154) | copy-start | bytes 774148
  124.7 6.6 %copy-start.32 = (f32[1,4,126,128]{3,2,1,0:T(8,128)}, f32[1,4,126,128]{3,2,1,0:T(8,128)S(1)}, u32[]{:S(2)}) copy-start(f32[1,4,126,128]{3,2,1,0:T(8,128)S(1)} %get-tuple-element.157) | copy-start | bytes 774148
  124.7 6.6 %copy-start.34 = (f32[1,4,126,128]{3,2,1,0:T(8,128)}, f32[1,4,126,128]{3,2,1,0:T(8,128)S(1)}, u32[]{:S(2)}) copy-start(f32[1,4,126,128]{3,2,1,0:T(8,128)S(1)} %get-tuple-element.166) | copy-start | bytes 774148
  124.7 6.6 %copy-start.52 = (f32[1,4,126,128]{3,2,1,0:T(8,128)}, f32[1,4,126,128]{3,2,1,0:T(8,128)S(1)}, u32[]{:S(2)}) copy-start(f32[1,4,126,128]{3,2,1,0:T(8,128)S(1)} %get-tuple-element.155) | copy-start | bytes 774148
  124.7 6.6 %copy-start.54 = (f32[1,4,126,128]{3,2,1,0:T(8,128)}, f32[1,4,126,128]{3,2,1,0:T(8,128)S(1)}, u32[]{:S(2)}) copy-start(f32[1,4,126,128]{3,2,1,0:T(8,128)S(1)} %get-tuple-element.156) | copy-start | bytes 774148
  124.7 6.6 %copy-start.56 = (f32[1,4,126,128]{3,2,1,0:T(8,128)}, f32[1,4,126,128]{3,2,1,0:T(8,128)S(1)}, u32[]{:S(2)}) copy-start(f32[1,4,126,128]{3,2,1,0:T(8,128)S(1)} %get-tuple-element.158) | copy-start | bytes 774148
  125.1 6.3 %copy-start.1 = (f32[1,4,127,128]{3,2,1,0:T(8,128)}, f32[1,4,127,128]{3,2,1,0:T(8,128)S(1)}, u32[]{:S(2)}) copy-start(f32[1,4,127,128]{3,2,1,0:T(8,128)S(1)} %get-tuple-element.176) | copy-start | bytes 780292
  125.1 6.3 %copy-start.3 = (f32[1,4,127,128]{3,2,1,0:T(8,128)}, f32[1,4,127,128]{3,2,1,0:T(8,128)S(1)}, u32[]{:S(2)}) copy-start(f32[1,4,127,128]{3,2,1,0:T(8,128)S(1)} %get-tuple-element.177) | copy-start | bytes 780292
  125.1 6.3 %copy-start.5 = (f32[1,4,127,128]{3,2,1,0:T(8,128)}, f32[1,4,127,128]{3,2,1,0:T(8,128)S(1)}, u32[]{:S(2)}) copy-start(f32[1,4,127,128]{3,2,1,0:T(8,128)S(1)} %get-tuple-element.179) | copy-start | bytes 780292
  125.1 6.3 %copy-start.16 = (f32[1,4,127,128]{3,2,1,0:T(8,128)}, f32[1,4,127,128]{3,2,1,0:T(8,128)S(1)}, u32[]{:S(2)}) copy-start(f32[1,4,127,128]{3,2,1,0:T(8,128)S(1)} %get-tuple-element.171) | copy-start | bytes 780292
  125.1 6.3 %copy-start.17 = (f32[1,4,127,128]{3,2,1,0:T(8,128)}, f32[1,4,127,128]{3,2,1,0:T(8,128)S(1)}, u32[]{:S(2)}) copy-start(f32[1,4,127,128]{3,2,1,0:T(8,128)S(1)} %get-tuple-element.173) | copy-start | bytes 780292
  125.1 6.3 %copy-start.24 = (f32[1,4,127,128]{3,2,1,0:T(8,128)}, f32[1,4,127,128]{3,2,1,0:T(8,128)S(1)}, u32[]{:S(2)}) copy-start(f32[1,4,127,128]{3,2,1,0:T(8,128)S(1)} %get-tuple-element.175) | copy-start | bytes 780292
  125.1 6.3 %copy-start.26 = (f32[1,4,127,128]{3,2,1,0:T(8,128)}, f32[1,4,127,128]{3,2,1,0:T(8,128)S(1)}, u32[]{:S(2)}) copy-start(f32[1,4,127,128]{3,2,1,0:T(8,128)S(1)} %get-tuple-element.178) | copy-start | bytes 780292
  125.1 6.3 %copy-start.36 = (f32[1,4,127,128]{3,2,1,0:T(8,128)}, f32[1,4,127,128]{3,2,1,0:T(8,128)S(1)}, u32[]{:S(2)}) copy-start(f32[1,4,127,128]{3,2,1,0:T(8,128)S(1)} %get-tuple-element.168) | copy-start | bytes 780292
  125.1 6.3 %copy-start.38 = (f32[1,4,127,128]{3,2,1,0:T(8,128)}, f32[1,4,127,128]{3,2,1,0:T(8,128)S(1)}, u32[]{:S(2)}) copy-start(f32[1,4,127,128]{3,2,1,0:T(8,128)S(1)} %get-tuple-element.169) | copy-start | bytes 780292
  125.1 6.3 %copy-start.40 = (f32[1,4,127,128]{3,2,1,0:T(8,128)}, f32[1,4,127,128]{3,2,1,0:T(8,128)S(1)}, u32[]{:S(2)}) copy-start(f32[1,4,127,128]{3,2,1,0:T(8,128)S(1)} %get-tuple-element.170) | copy-start | bytes 780292
  125.2 6.3 %copy-start.42 = (f32[1,4,127,128]{3,2,1,0:T(8,128)}, f32[1,4,127,128]{3,2,1,0:T(8,128)S(1)}, u32[]{:S(2)}) copy-start(f32[1,4,127,128]{3,2,1,0:T(8,128)S(1)} %get-tuple-element.174) | copy-start | bytes 780292
  125.2 10.2 %copy-start.58 = (f32[1,4,127,128]{3,2,1,0:T(8,128)}, f32[1,4,127,128]{3,2,1,0:T(8,128)S(1)}, u32[]{:S(2)}) copy-start(f32[1,4,127,128]{3,2,1,0:T(8,128)S(1)} %get-tuple-element.172) | copy-start | bytes 780292
  125.2 10.2 %copy-start.60 = (f32[1,4,127,128]{3,2,1,0:T(8,128)}, f32[1,4,127,128]{3,2,1,0:T(8,128)S(1)}, u32[]{:S(2)}) copy-start(f32[1,4,127,128]{3,2,1,0:T(8,128)S(1)} %get-tuple-element.180) | copy-start | bytes 780292
  125.2 10.2 %copy-start.74 = (f32[1,4,3,128]{3,2,1,0:T(4,128)}, f32[1,4,3,128]{3,2,1,0:T(4,128)S(1)}, u32[]{:S(2)}) copy-start(f32[1,4,3,128]{3,2,1,0:T(4,128)S(1)} %get-tuple-element.134) | copy-start | bytes 18436
  125.2 10.2 %copy-start.76 = (f32[1,4,3,128]{3,2,1,0:T(4,128)}, f32[1,4,3,128]{3,2,1,0:T(4,128)S(1)}, u32[]{:S(2)}) copy-start(f32[1,4,3,128]{3,2,1,0:T(4,128)S(1)} %get-tuple-element.135) | copy-start | bytes 18436
  125.2 10.2 %copy-start.78 = (f32[1,4,3,128]{3,2,1,0:T(4,128)}, f32[1,4,3,128]{3,2,1,0:T(4,128)S(1)}, u32[]{:S(2)}) copy-start(f32[1,4,3,128]{3,2,1,0:T(4,128)S(1)} %get-tuple-element.136) | copy-start | bytes 18436
  131.4 4.2 copy-start.84
  139.7 34.9 %all-to-all-start = ((bf16[16,1,69,4,128]{4,3,2,1,0:T(4,128)(2,1)}), bf16[16,1,69,4,128]{4,3,2,1,0:T(4,128)(2,1)}, u32[]{:S(2)}, u32[]{:S(2)}) async-start(bf16[16,1,69,4,128]{4,3,2,1,0:T(4,128)(2,1)} %stack.153), calls=%async_computation | async-start | bytes 2260992 | tf_op jit(solution)/shard_map/all_to_all | solution.py:172
  144.5 177.4 %reduce-scatter.5.cloned.1.call-start = ((), (), s32[]{:S(2)}) async-start(), calls=%async_computation.4 | async-start | bytes 270336 | tf_op jit(solution)/shard_map/reduce_scatter | solution.py:221
  192.2 3.9 copy-start.71
  196.1 3.3 copy-start.57
  204.8 242.1 %reduce-scatter.3.cloned.1.call-start = ((), (), s32[]{:S(2)}) async-start(), calls=%async_computation.3 | async-start | bytes 270336 | tf_op jit(solution)/shard_map/reduce_scatter | solution.py:220
  (62 other events, 100.7 us)
Sparse Core Ops, SparseCore 0:
  204.9 116.9 reduce-scatter.4
  326.5 120.3 reduce-scatter.2
